TPU v7x, 512 devices: a whole 4x4x16 slice. The times are simulated.
512 devices in a mesh: seq: 32 (over z, core), dp: 16 (over x, y).
Axes of the slice: x: 4, y: 4, z: 16, core: 2. Of those that a mesh axis runs over, the one named last changes fastest.
Arguments:
- queries: bfloat16 [16, 5120, 2048], P('dp', 'seq'), may hold values from -6 to 6
- keys: bfloat16 [16, 5120, 2048], P('dp', 'seq'), may hold values from -6 to 6
- values: bfloat16 [16, 5120, 2048], P('dp', 'seq'), may hold values from -6 to 6
- keep: int32 [16, 5120, 2048], P('dp', 'seq'), may hold values 0 or 1
- gain: float32 [2048], replicated, may hold values from 0.25 to 1.75
- out_weight: bfloat16 [2048, 2048], P(None, 'dp'), may hold values from -0.125 to 0.125
Outputs:
- projected: bfloat16 [16, 5120, 2048], P('dp', 'seq')
All inputs are finite; a program needn't handle non-finite values. No bound on the sum of `keep` on one device may be relied on, other than what follows from the above.
Results may differ from a plain program's by a relative error of at most 0.0051.
Values may be sent and summed in bfloat16 or wider, within the bound.
No kernel may reach another device: no remote copies, remote signals or barrier semaphores. Data moves between devices by JAX's collectives and lax.ppermute only.
A program may use at most 128 MiB of HBM per device.

v0:
```python
import jax
import jax.numpy as jnp
from jax import lax
from jax.sharding import PartitionSpec as P

HEADS = 16
HEAD = 128


def prefix_2(x, axis, combine, identity):
    size, place = (lax.axis_size(axis), lax.axis_index(axis))
    everything = lax.all_gather(x, axis)
    start = jnp.broadcast_to(jnp.asarray(identity, x.dtype), x.shape)

    def turn(k, before):
        reached = k < place
        new = combine(before, everything[k])
        return jnp.where(reached, new, before)

    return lax.fori_loop(0, size, turn, start)


def feature(x):
    xf = x.astype(jnp.float32)
    return jnp.where(xf > 0, xf + 1.0, jnp.exp(jnp.minimum(xf, 0.0))).astype(jnp.bfloat16)


def add_states(earlier, later):
    return earlier + later


def on_device(queries, keys, values, keep, gain, out_weight):
    tok_rows = queries.shape[1]
    fq = feature(queries[0]).reshape(tok_rows, HEADS, HEAD)
    fk = feature(keys[0]).reshape(tok_rows, HEADS, HEAD)
    vals = values[0].reshape(tok_rows, HEADS, HEAD)
    state = jnp.einsum("thc,thd->hcd", fk, vals, preferred_element_type=jnp.float32)
    prefix = prefix_2(state, "seq", add_states, jnp.zeros_like(state))
    prefix = prefix.astype(jnp.bfloat16)
    inter = jnp.einsum("thc,hcd->thd", fq, prefix, preferred_element_type=jnp.float32)
    causal = jnp.arange(tok_rows)[:, None] >= jnp.arange(tok_rows)[None, :]
    scores = jnp.einsum("thc,shc->hts", fq, fk, preferred_element_type=jnp.float32)
    scores = jnp.where(causal[None], scores, 0.0).astype(jnp.bfloat16)
    intra = jnp.einsum("hts,shd->thd", scores, vals, preferred_element_type=jnp.float32)
    numer = inter + intra
    normed = (
        numer
        * lax.rsqrt(jnp.mean(numer * numer, axis=-1, keepdims=True) + 1e-06)
        * gain.reshape(HEADS, HEAD)
    )
    mask = keep[0].reshape(tok_rows, HEADS, HEAD).astype(jnp.float32)
    dropped = (normed * mask * (1.0 / 0.9)).astype(jnp.bfloat16).reshape(tok_rows, HEADS * HEAD)
    result = jnp.dot(
        dropped,
        lax.all_gather(out_weight, "dp", axis=1, tiled=True),
        preferred_element_type=jnp.float32,
    ).astype(jnp.bfloat16)
    return result[None]


def solution(mesh):
    return jax.shard_map(
        on_device,
        mesh=mesh,
        in_specs=(
            P("dp", "seq", None),
            P("dp", "seq", None),
            P("dp", "seq", None),
            P("dp", "seq", None),
            P(),
            P(None, "dp"),
        ),
        out_specs=P("dp", "seq", None),
        check_vma=False,
    )
```

profile of v0, /device:TPU:6, one launch (start us, length us, event | category | flops | bytes accessed | tf_op | source)
XLA Modules:
  0.0 312.9 jit_solution(7465845264773032418)
XLA Ops:
  14.4 3.3 %fusion.3 = f32[160,16,128]{2,0,1:T(8,128)} fusion(pred[160,160]{1,0:T(8,128)(4,1)S(1)} %iota_compare_fusion, bf16[160,16,128]{2,1,0:T(8,128)(2,1)} %bitcast.42, bf16[160,16,128]{2,1,0:T(8,128)(2,1)} %bitcast.41, bf16[160,16,128]{2,1,0:T(8,128)(2,1)S(1)} %bitcast.39), kind=kOutput, calls=%fused_computation.13 | convolution fusion | flops 210534400 | bytes 3302400 | tf_op jit(solution)/shard_map/hts,shd->thd/dot_general | solution.py:44
  17.7 188.8 %all-gather.6.cloned.1.call-done = f32[512,128,128]{2,1,0:T(8,128)} async-done(((f32[16,128,128]{2,1,0:T(8,128)}), f32[512,128,128]{2,1,0:T(8,128)}) %all-gather.6.cloned.1.call-update) | async-done | bytes 33554448 | tf_op jit(solution)/shard_map/all_gather | solution.py:12
  206.4 51.9 %while.14 = (s32[]{:T(128)}, f32[16,128,128]{2,1,0:T(8,128)S(1)}, s32[]{:T(128)}, f32[32,16,128,128]{3,2,1,0:T(8,128)}, s32[]{:T(128)}, /*index=5*/s32[]{:T(128)}) while((s32[]{:T(128)}, f32[16,128,128]{2,1,0:T(8,128)S(1)}, s32[]{:T(128)}, f32[32,16,128,128]{3,2,1,0:T(8,128)}, s32[]{:T(128)}, /*index=5*/s32[]{:T(128)}) %tuple.40), condition=%wide.region_1.2_spmd.clone, body=%wide.region_0.1_spmd.clone.sunk | while | flops 786436 | bytes 3145821 | solution.py:20
  206.4 1.7 add_select_fusion.2
  208.1 1.6 add_select_fusion.2
  213.0 1.6 add_select_fusion.2
  214.6 1.6 add_select_fusion.2
  216.2 1.6 add_select_fusion.2
  221.0 1.6 add_select_fusion.2
  222.6 1.6 add_select_fusion.2
  224.3 1.7 add_select_fusion.2
  225.9 1.6 add_select_fusion.2
  227.6 1.6 add_select_fusion.2
  229.2 1.6 add_select_fusion.2
  230.8 1.6 add_select_fusion.2
  232.5 1.6 add_select_fusion.2
  234.1 1.6 add_select_fusion.2
  235.7 1.6 add_select_fusion.2
  237.3 1.6 add_select_fusion.2
  240.6 1.6 add_select_fusion.2
  242.2 1.6 add_select_fusion.2
  258.4 3.1 multiply_reduce_fusion
  261.4 38.1 %all-gather.4.cloned.1.call-done = bf16[2048,2048]{1,0:T(8,128)(2,1)} async-done(((bf16[2048,128]{1,0:T(8,128)(2,1)}), bf16[2048,2048]{1,0:T(8,128)(2,1)}) %all-gather.4.cloned.1.call-update) | async-done | bytes 8388624 | tf_op jit(solution)/shard_map/all_gather | solution.py:55
  299.5 6.6 %fusion = bf16[1,160,2048]{2,1,0:T(8,128)(2,1)} fusion(bf16[2048,2048]{1,0:T(8,128)(2,1)} %all-gather.4.cloned.1.call-done, f32[160,16,128]{2,1,0:T(8,128)S(1)} %bitcast.37, f32[160,16,128]{2,0,1:T(8,128)} %get-tuple-element.109, f32[16,128]{1,0:T(8,128)S(1)} %bitcast.46, f32[160,16]{0,1:T(8,128)S(1)} %add_rsqrt_fusion), kind=kOutput, calls=%fused_computation.3 | convolution fusion | flops 1344143360 | bytes 11683840 | tf_op jit(solution)/shard_map/dot_general | solution.py:53
  (39 shorter events, 30.0 us)
Async XLA Ops:
  6.5 1.6 copy-start.3
  6.5 199.9 %all-gather.6.cloned.1.call-start = ((), (), s32[]{:S(2)}) async-start(), calls=%async_computation.1 | async-start | bytes 34603008 | tf_op jit(solution)/shard_map/all_gather | solution.py:12
  8.3 0.9 copy-start
  10.7 288.8 %all-gather.4.cloned.1.call-start = ((), (), s32[]{:S(2)}) async-start(), calls=%async_computation | async-start | bytes 8912896 | tf_op jit(solution)/shard_map/all_gather | solution.py:55
  11.5 2.5 copy-start.2
  206.4 51.9 %copy-start.1 = (bf16[20,8,16,128]{3,2,1,0:T(8,128)(2,1)S(1)}, bf16[20,8,16,128]{3,2,1,0:T(8,128)(2,1)}, u32[]{:S(2)}) copy-start(bf16[20,8,16,128]{3,2,1,0:T(8,128)(2,1)} %copy.26) | copy-start | bytes 1966084
  258.4 41.2 %copy-start.4 = (f32[2048]{0:T(1024)S(1)}, f32[2048]{0:T(1024)}, u32[]{:S(2)}) copy-start(f32[2048]{0:T(1024)} %param.12) | copy-start | bytes 24580
Sparse Core Ops, SparseCore 0:
  10.8 195.5 all-gather.5
  209.4 90.0 all-gather.3
where the time goes:
time: 314 us; the launch traced here: 313 us
  waiting for transfers between devices  228 us (73%)
  other arithmetic  54.3 us (17%)
  matrix products  14.4 us (5%)
  between operations  13.5 us (4%)
    all_gather x1, waiting for transfers between devices, prefix_2(): everything = lax.all_gather(x, axis)  189 us
    select_n x32, other arithmetic, turn(): return jnp.where(reached, new, before)  51.1 us
    all_gather x1, waiting for transfers between devices, on_device(): lax.all_gather(out_weight, 'dp', axis=1, tiled=True)  38.1 us
    dot_general x1, matrix products, on_device(): jnp.dot(dropped, lax.all_gather(out_weight, 'dp', axis=1, tiled=True), pr...  6.56 us
  transfers between devices with their start and end apart: 2, of which 2 were waited for; matrix products, arithmetic and copies ran while one was open for 19% of the time, Pallas kernels for 0%

commit v1 on v0

v1 whole, which is shorter than its diff:
```python
import jax
import jax.numpy as jnp
import numpy as np
from jax import lax
from jax.experimental import pallas as pl
from jax.experimental.pallas import tpu as pltpu
from jax.sharding import PartitionSpec as P

HEADS = 16
HEAD = 128
HALF = 8
TOK = 160
HC = 2048
F32 = jnp.float32
BF16 = jnp.bfloat16
SWAP = [(0, 1), (1, 0)]


def feature(x):
    xf = x.astype(F32)
    return jnp.where(xf > 0, xf + 1.0, jnp.exp(jnp.minimum(xf, 0.0))).astype(BF16)


def dot(a, b, contract):
    return lax.dot_general(a, b, (contract, ((), ())), preferred_element_type=F32)


def state_kernel(core, k, v, send, own):
    step = pl.program_id(0)
    for h in range(4):
        cols = slice(h * HEAD, (h + 1) * HEAD)
        s = dot(feature(k[:, cols]), v[:, cols], ((0,), (0,)))

        @pl.when(step < 2)
        def _():
            send[h] = s.astype(BF16)

        @pl.when(step >= 2)
        def _():
            own[h] = s


def block_states(core, keys, values):
    def half(i, core):
        return jnp.where(i < 2, 1 - core[0], core[0]) * 2 + i % 2

    spec = pl.BlockSpec((TOK, 512), lambda i, core: (0, half(i, core)))
    return pl.pallas_call(
        state_kernel,
        grid_spec=pltpu.PrefetchScalarGridSpec(
            num_scalar_prefetch=1,
            grid=(4,),
            in_specs=[spec, spec],
            out_specs=[
                pl.BlockSpec((4, HEAD, HEAD), lambda i, core: (jnp.minimum(i, 1), 0, 0)),
                pl.BlockSpec((4, HEAD, HEAD), lambda i, core: (jnp.maximum(i - 2, 0), 0, 0)),
            ],
        ),
        out_shape=[
            jax.ShapeDtypeStruct((HALF, HEAD, HEAD), BF16),
            jax.ShapeDtypeStruct((HALF, HEAD, HEAD), F32),
        ],
        name="block_states",
    )(core, keys, values)


def scan_kernel(x, y):
    run = jnp.zeros(x.shape[1:], F32)
    for z in range(x.shape[0]):
        y[z] = run.astype(BF16)
        run = run + x[z].astype(F32)


def scan_chips(x):
    return pl.pallas_call(scan_kernel, out_shape=jax.ShapeDtypeStruct(x.shape, BF16), name="scan_chips")(x)


def heads_kernel(core, q, k, v, keep, gain, mine, theirs, out):
    step = pl.program_id(0)
    row = lax.broadcasted_iota(jnp.int32, (TOK, TOK), 0)
    col = lax.broadcasted_iota(jnp.int32, (TOK, TOK), 1)
    causal = row >= col
    for h in range(4):
        cols = slice(h * HEAD, (h + 1) * HEAD)
        fq = feature(q[:, cols])
        fk = feature(k[:, cols])
        prefix = jnp.where(step < 2, mine[h].astype(F32), theirs[h].astype(F32)).astype(BF16)
        scores = dot(fq, fk, ((1,), (1,)))
        scores = jnp.where(causal, scores, 0.0).astype(BF16)
        numer = dot(fq, prefix, ((1,), (0,))) + dot(scores, v[:, cols], ((1,), (0,)))
        mean = jnp.mean(numer * numer, axis=-1, keepdims=True)
        normed = numer * lax.rsqrt(mean + 1e-06) * gain[:, cols]
        out[:, cols] = (normed * keep[:, cols].astype(F32) * (1.0 / 0.9)).astype(BF16)


def heads(core, q, k, v, keep, gain, mine, theirs):
    def half(i, core):
        return jnp.where(i < 2, core[0], 1 - core[0]) * 2 + i % 2

    spec = pl.BlockSpec((TOK, 512), lambda i, core: (0, half(i, core)))
    state = pl.BlockSpec((4, HEAD, HEAD), lambda i, core: (i % 2, 0, 0))
    return pl.pallas_call(
        heads_kernel,
        grid_spec=pltpu.PrefetchScalarGridSpec(
            num_scalar_prefetch=1,
            grid=(4,),
            in_specs=[spec, spec, spec, spec, pl.BlockSpec((1, 512), lambda i, core: (0, half(i, core))), state, state],
            out_specs=spec,
        ),
        out_shape=jax.ShapeDtypeStruct((TOK, HC), BF16),
        name="heads",
    )(core, q, k, v, keep, gain, mine, theirs)


def project_kernel(x, top, bottom, out):
    acc = dot(x[:, : HC // 2], top[...], ((1,), (0,)))
    acc += dot(x[:, HC // 2 :], bottom[...], ((1,), (0,)))
    out[...] = acc.astype(BF16)


def project(dropped, weight):
    wide = 512
    return pl.pallas_call(
        project_kernel,
        grid=(HC // wide,),
        in_specs=[
            pl.BlockSpec((TOK, HC), lambda i: (0, 0)),
            pl.BlockSpec((HC // 2, wide), lambda i: (0, i)),
            pl.BlockSpec((HC // 2, wide), lambda i: (0, i + HC // wide)),
        ],
        out_specs=pl.BlockSpec((TOK, wide), lambda i: (0, i)),
        out_shape=jax.ShapeDtypeStruct((TOK, HC), BF16),
        name="project",
    )(dropped, weight, weight)


def on_device(queries, keys, values, keep, gain, out_weight):
    place = lax.axis_index("core")
    core = place.astype(jnp.int32).reshape(1)
    part = lax.dynamic_slice_in_dim(out_weight, place * (HC // 2), HC // 2, 0)
    weight = lax.all_gather(part, ("core", "x", "y"), axis=1, tiled=True)

    send, own = block_states(core, keys[0], values[0])
    other = lax.ppermute(send, "core", SWAP)
    chip = (own + other.astype(F32)).astype(BF16).reshape(16, HEAD // 2, HEAD)
    slices = lax.all_to_all(chip, "z", 0, 0)
    before = lax.all_to_all(scan_chips(slices), "z", 0, 0).reshape(HALF, HEAD, HEAD)
    before = before.astype(F32)
    first = place == 0
    there = (before + jnp.where(first, own, 0.0)).astype(BF16)
    mine = (before + jnp.where(first, 0.0, other.astype(F32))).astype(BF16)
    theirs = lax.ppermute(there, "core", SWAP)
    dropped = heads(core, queries[0], keys[0], values[0], keep[0], gain.reshape(1, HC), mine, theirs)
    return project(dropped, weight)[None]


def solution(mesh):
    fine = jax.sharding.Mesh(np.asarray(mesh.devices).reshape(16, 2, 4, 4), ("z", "core", "x", "y"))
    tokens = P(("x", "y"), ("z", "core"), None)
    return jax.shard_map(
        on_device,
        mesh=fine,
        in_specs=(tokens, tokens, tokens, tokens, P(), P(None, ("x", "y"))),
        out_specs=tokens,
        check_vma=False,
    )
```

time: 314 us -> 105 us (0.33)
  waiting for transfers between devices: 228 us -> 21.6 us
  other arithmetic: 54.3 us -> 2.99 us
  blocking collectives: 0 us -> 33.6 us
  Pallas kernels: 0 us -> 19.3 us
  matrix products: 14.4 us -> 0 us
  starting transfers between devices: 0.04 us -> 9.77 us
    all_gather x2 -> x1, waiting for transfers between devices: 227 us -> 0.01 us  [on_device(): weight = lax.all_gather(part, ('core', 'x', 'y'), axis=1, tiled=True)]
    select_n x32 -> x0, other arithmetic: 51.1 us -> none  [turn(): return jnp.where(reached, new, before)]
    all_to_all x0 -> x1, blocking collectives: none -> 33.6 us  [on_device(): slices = lax.all_to_all(chip, 'z', 0, 0)]
    pallas_call x0 -> x4, Pallas kernels: none -> 19.3 us  [the longest x1 6.23 us: project(): pl.pallas_call(project_kernel, grid=(HC // wide,), in_specs=[pl.BlockSpec...]
    all_to_all x0 -> x1, waiting for transfers between devices: none -> 18.3 us  [on_device(): lax.all_to_all(scan_chips(slices), 'z', 0, 0).reshape(HALF, HEAD, HEAD)]
    dot_general x4 -> x0, matrix products: 14.4 us -> none  [the longest x1 6.56 us: on_device(): jnp.dot(dropped, lax.all_gather(out_weight, 'dp', axis=1, tiled=True), pr...]
    all_to_all x0 -> x1, starting transfers between devices: none -> 5.95 us  [on_device(): lax.all_to_all(scan_chips(slices), 'z', 0, 0).reshape(HALF, HEAD, HEAD)]
    ppermute x0 -> x2, starting transfers between devices: none -> 3.82 us  [the longest x1 1.91 us: on_device(): theirs = lax.ppermute(there, 'core', SWAP)]
  transfers between devices with their start and end apart: 2 -> 4, of which waited for: 2 -> 3; matrix products, arithmetic and copies ran while one was open for 19% -> 3% of each run, Pallas kernels for 0% -> 13%
where the time goes in v1:
time: 105 us; the launch traced here: 103 us
  blocking collectives  33.6 us (32%)
  waiting for transfers between devices  21.6 us (21%)
  Pallas kernels  19.3 us (18%)
  between operations  13.4 us (13%)
  starting transfers between devices  9.77 us (9%)
  other arithmetic  2.99 us (3%)
  local copies, waits for them, and re-layouts  2.49 us (2%)
    all_to_all x1, blocking collectives, on_device(): slices = lax.all_to_all(chip, 'z', 0, 0)  33.6 us
    all_to_all x1, waiting for transfers between devices, on_device(): lax.all_to_all(scan_chips(slices), 'z', 0, 0).reshape(HALF, HEAD, HEAD)  18.3 us
    pallas_call x1, Pallas kernels, project(): pl.pallas_call(project_kernel, grid=(HC // wide,), in_specs=[pl.BlockSpec...  6.23 us
    all_to_all x1, starting transfers between devices, on_device(): lax.all_to_all(scan_chips(slices), 'z', 0, 0).reshape(HALF, HEAD, HEAD)  5.95 us
    pallas_call x1, Pallas kernels, heads(): pl.pallas_call(heads_kernel, grid_spec=pltpu.PrefetchScalarGridSpec(num_s...  5.87 us
    pallas_call x1, Pallas kernels, block_states(): pl.pallas_call(state_kernel, grid_spec=pltpu.PrefetchScalarGridSpec(num_s...  5.49 us
  transfers between devices with their start and end apart: 4, of which 3 were waited for; matrix products, arithmetic and copies ran while one was open for 3% of the time, Pallas kernels for 13%

profile of v1, /device:TPU:6, one launch (start us, length us, event | category | flops | bytes accessed | tf_op | source)
XLA Modules:
  0.0 103.1 jit_solution(8693543186055617891)
XLA Ops:
  6.5 0.0 copy-start
  6.5 0.0 all-gather.2.cloned.1.call-start
  6.5 1.0 %copy-done = bf16[2048,128]{1,0:T(8,128)(2,1)S(1)} copy-done((bf16[2048,128]{1,0:T(8,128)(2,1)S(1)}, bf16[2048,128]{1,0:T(8,128)(2,1)}, u32[]{:S(2)}) %copy-start) | copy-done | bytes 524312
  7.6 0.7 constant_dynamic-slice_fusion
  8.3 0.0 all-gather.2.cloned.1.call-update
  8.3 5.5 %block_states.1 = (bf16[8,128,128]{2,1,0:T(8,128)(2,1)}, f32[8,128,128]{2,1,0:T(8,128)}) custom-call(s32[1]{0:T(128)} %bitcast.core, bf16[160,2048]{1,0:T(8,128)(2,1)} %bitcast.13, bf16[160,2048]{1,0:T(8,128)(2,1)} %bitcast.15), custom_call_target="tpu_custom_call" | custom-call | tf_op jit(solution)/shard_map/block_states/pallas_call | solution.py:48
  13.8 1.9 %collective-permute-start = (bf16[8,128,128]{2,1,0:T(8,128)(2,1)}, bf16[8,128,128]{2,1,0:T(8,128)(2,1)S(1)}, u32[]{:S(2)}, u32[]{:S(2)}) collective-permute-start(bf16[8,128,128]{2,1,0:T(8,128)(2,1)} %get-tuple-element.8), channel_id=1, source_target_pairs={{0,16},{16,0},{1,17},{17,1},{2,18},{18,2},{3,19},{19,3},{4,20},{20... | collective-permute-start | bytes 786440 | tf_op jit(solution)/shard_map/ppermute | solution.py:144
  15.8 1.7 %collective-permute-done = bf16[8,128,128]{2,1,0:T(8,128)(2,1)S(1)} collective-permute-done((bf16[8,128,128]{2,1,0:T(8,128)(2,1)}, bf16[8,128,128]{2,1,0:T(8,128)(2,1)S(1)}, u32[]{:S(2)}, u32[]{:S(2)}) %collective-permute-start) | collective-permute-done | bytes 262176 | tf_op jit(solution)/shard_map/ppermute | solution.py:144
  17.5 1.1 %fusion = bf16[8,128,128]{2,1,0:T(8,128)(2,1)S(1)} fusion(f32[8,128,128]{2,1,0:T(8,128)} %get-tuple-element.7, bf16[8,128,128]{2,1,0:T(8,128)(2,1)S(1)} %collective-permute-done), kind=kLoop, calls=%fused_computation.4 | loop fusion | flops 393216 | bytes 1048576 | tf_op jit(solution)/shard_map/convert_element_type | solution.py:145
  18.6 33.6 %all_to_all.10.x = bf16[16,64,128]{2,1,0:T(8,128)(2,1)} all-to-all(bf16[16,64,128]{2,1,0:T(8,128)(2,1)S(1)} %bitcast.19), channel_id=1, replica_groups=mesh['z'=16,'core'=2,'x'=4,'y'=4] {'z'}, dimensions={0} | all-to-all | bytes 524288 | tf_op jit(solution)/shard_map/all_to_all | solution.py:146
  52.2 1.7 %scan_chips.1 = bf16[16,64,128]{2,1,0:T(8,128)(2,1)} custom-call(bf16[16,64,128]{2,1,0:T(8,128)(2,1)} %all_to_all.10.x), custom_call_target="tpu_custom_call" | custom-call | tf_op jit(solution)/shard_map/scan_chips/pallas_call | solution.py:75
  53.9 6.0 %all-to-all-start.1 = ((bf16[16,64,128]{2,1,0:T(8,128)(2,1)}), bf16[16,64,128]{2,1,0:T(8,128)(2,1)S(1)}, u32[]{:S(2)}, u32[]{:S(2)}) async-start(bf16[16,64,128]{2,1,0:T(8,128)(2,1)} %scan_chips.1), calls=%async_computation.1 | async-start | bytes 524288 | tf_op jit(solution)/shard_map/all_to_all | solution.py:147
  59.8 18.3 %all-to-all-done.1 = bf16[16,64,128]{2,1,0:T(8,128)(2,1)S(1)} async-done(((bf16[16,64,128]{2,1,0:T(8,128)(2,1)}), bf16[16,64,128]{2,1,0:T(8,128)(2,1)S(1)}, u32[]{:S(2)}, u32[]{:S(2)}) %all-to-all-start.1) | async-done | bytes 262176 | tf_op jit(solution)/shard_map/all_to_all | solution.py:147
  78.2 1.9 %fusion.2 = (bf16[8,128,128]{2,1,0:T(8,128)(2,1)S(1)}, bf16[8,128,128]{2,1,0:T(8,128)(2,1)}) fusion(f32[8,128,128]{2,1,0:T(8,128)} %get-tuple-element.7, pred[]{:T(512)S(6)} %eq.3, bf16[8,128,128]{2,1,0:T(8,128)(2,1)S(1)} %collective-permute-done, bf16[8,128,128]{2,1,0:T(8,128)(2,1)S(1)} %bitcast.18), kind=kLoop, calls=%fused_computation.6 | loop fusion | flops 1048576 | bytes 1572865 | tf_op jit(solution)/shard_map/convert_element_type | solution.py:150
  80.1 1.9 %collective-permute-start.1 = (bf16[8,128,128]{2,1,0:T(8,128)(2,1)S(1)}, bf16[8,128,128]{2,1,0:T(8,128)(2,1)S(1)}, u32[]{:S(2)}, u32[]{:S(2)}) collective-permute-start(bf16[8,128,128]{2,1,0:T(8,128)(2,1)S(1)} %get-tuple-element.9), channel_id=1, source_target_pairs={{0,16},{16,0},{1,17},{17,1},{2,18},{18,2},{3,19},{19,3},{4,20},{20... | collective-permute-start | bytes 786440 | tf_op jit(solution)/shard_map/ppermute | solution.py:152
  82.0 1.5 %collective-permute-done.1.theirs = bf16[8,128,128]{2,1,0:T(8,128)(2,1)S(1)} collective-permute-done((bf16[8,128,128]{2,1,0:T(8,128)(2,1)S(1)}, bf16[8,128,128]{2,1,0:T(8,128)(2,1)S(1)}, u32[]{:S(2)}, u32[]{:S(2)}) %collective-permute-start.1) | collective-permute-done | bytes 262176 | tf_op jit(solution)/shard_map/ppermute | solution.py:152
  83.5 0.0 copy-start.1
  83.5 0.7 copy-done.1
  84.2 5.9 %heads.1.x = bf16[160,2048]{1,0:T(8,128)(2,1)} custom-call(s32[1]{0:T(128)} %bitcast.core, bf16[160,2048]{1,0:T(8,128)(2,1)} %bitcast.20, bf16[160,2048]{1,0:T(8,128)(2,1)} %bitcast.14, bf16[160,2048]{1,0:T(8,128)(2,1)} %bitcast.16, s32[160,2048]{1,0:T(8,128)} %bitcast.17, f32[1,2048]{1,0:T(1,128)} %bitcast.21, bf16[8,128,128]{2,1,0:T(8,128)(2,1)} %get-tuple-element.10.mine, ...), custom_call_target="tpu_custom_call" | custom-call | tf_op jit(solution)/shard_map/heads/pallas_call | solution.py:102
  90.1 0.0 all-gather.2.cloned.1.call-done.top.bottom
  90.1 6.2 %project.1 = bf16[160,2048]{1,0:T(8,128)(2,1)} custom-call(bf16[160,2048]{1,0:T(8,128)(2,1)} %heads.1.x, bf16[1024,4096]{1,0:T(8,128)(2,1)} %all-gather.2.cloned.1.call-done.top.bottom, bf16[1024,4096]{1,0:T(8,128)(2,1)} %all-gather.2.cloned.1.call-done.top.bottom), custom_call_target="tpu_custom_call" | custom-call | tf_op jit(solution)/shard_map/project/pallas_call | solution.py:123
Async XLA Ops:
  6.5 1.0 %copy-start = (bf16[2048,128]{1,0:T(8,128)(2,1)S(1)}, bf16[2048,128]{1,0:T(8,128)(2,1)}, u32[]{:S(2)}) copy-start(bf16[2048,128]{1,0:T(8,128)(2,1)} %param.11) | copy-start | bytes 1572868
  6.5 83.5 %all-gather.2.cloned.1.call-start = ((), (), s32[]{:S(2)}) async-start(), calls=%async_computation.2 | async-start | bytes 8650752 | tf_op jit(solution)/shard_map/all_gather | solution.py:141
  13.8 3.6 %collective-permute-start = (bf16[8,128,128]{2,1,0:T(8,128)(2,1)}, bf16[8,128,128]{2,1,0:T(8,128)(2,1)S(1)}, u32[]{:S(2)}, u32[]{:S(2)}) collective-permute-start(bf16[8,128,128]{2,1,0:T(8,128)(2,1)} %get-tuple-element.8), channel_id=1, source_target_pairs={{0,16},{16,0},{1,17},{17,1},{2,18},{18,2},{3,19},{19,3},{4,20},{20... | collective-permute-start | bytes 786440 | tf_op jit(solution)/shard_map/ppermute | solution.py:144
  53.9 24.3 %all-to-all-start.1 = ((bf16[16,64,128]{2,1,0:T(8,128)(2,1)}), bf16[16,64,128]{2,1,0:T(8,128)(2,1)S(1)}, u32[]{:S(2)}, u32[]{:S(2)}) async-start(bf16[16,64,128]{2,1,0:T(8,128)(2,1)} %scan_chips.1), calls=%async_computation.1 | async-start | bytes 524288 | tf_op jit(solution)/shard_map/all_to_all | solution.py:147
  80.1 3.4 %collective-permute-start.1 = (bf16[8,128,128]{2,1,0:T(8,128)(2,1)S(1)}, bf16[8,128,128]{2,1,0:T(8,128)(2,1)S(1)}, u32[]{:S(2)}, u32[]{:S(2)}) collective-permute-start(bf16[8,128,128]{2,1,0:T(8,128)(2,1)S(1)} %get-tuple-element.9), channel_id=1, source_target_pairs={{0,16},{16,0},{1,17},{17,1},{2,18},{18,2},{3,19},{19,3},{4,20},{20... | collective-permute-start | bytes 786440 | tf_op jit(solution)/shard_map/ppermute | solution.py:152
  83.5 0.7 copy-start.1
Sparse Core Ops, SparseCore 0:
  10.4 77.8 all-gather.1
